TPU v7x, 32 devices: a whole 2x2x4 slice. The times are simulated.
32 devices in a mesh: grp: 2 (over y), row: 4 (over z), col: 4 (over x, core).
Axes of the slice: x: 2, y: 2, z: 4, core: 2. Of those that a mesh axis runs over, the one named last changes fastest.
Arguments:
- factor: float32 [4, 1024, 1024], P('grp', ('row', 'col')), may hold values from -0.1875 to 0.1875
- pivots: float32 [4, 1024], P('grp', ('row', 'col')), may hold values from 0.5 to 2
- constraints: float32 [4, 1024, 4096], P('grp', None, ('col', 'row')), may hold values from -0.09375 to 0.09375
Outputs:
- q_panels: float32 [4, 1024, 4096], P('row', 'grp', 'col')
All inputs are finite; a program needn't handle non-finite values.
Results may differ from a plain program's by a relative error of at most 0.0011.
Values may be sent and summed in bfloat16 or wider, within the bound.
A program may use at most 64 MiB of HBM per device.

v0:
```python
import jax
import jax.numpy as jnp
from jax import lax
from jax.sharding import PartitionSpec as P

exact_mode = lax.Precision.HIGHEST


def body(factor, pivots, constraints):
    factor_piece = lax.all_gather(factor, ("row", "col"), axis=1, tiled=True)
    pivot_piece = lax.all_gather(pivots, ("row", "col"), axis=1, tiled=True)
    row_ids = lax.broadcasted_iota(jnp.int32, factor_piece.shape, 1)
    col_ids = lax.broadcasted_iota(jnp.int32, factor_piece.shape, 2)
    triangle = jnp.where(col_ids < row_ids, factor_piece, jnp.zeros_like(factor_piece))
    product = jnp.einsum(
        "brm,bms->brs",
        triangle,
        constraints,
        precision=exact_mode,
        preferred_element_type=jnp.float32,
    )
    scaled = pivot_piece[:, :, None] * constraints
    projected_full = product + scaled
    projected = projected_full.astype(jnp.bfloat16)
    column_panel = lax.all_gather(projected, "row", axis=2, tiled=True)
    gram_tile = lax.dot_general(
        lax.all_gather(projected, "col", axis=2, tiled=True),
        column_panel,
        (((0, 1), (0, 1)), ((), ())),
        preferred_element_type=jnp.float32,
    )
    summed = lax.psum_scatter(gram_tile, "grp", scatter_dimension=0, tiled=True)
    return summed[None]


def solution(mesh):
    in_specs = (
        P("grp", ("row", "col"), None),
        P("grp", ("row", "col")),
        P("grp", None, ("col", "row")),
    )
    out_specs = P("row", "grp", "col")
    return jax.shard_map(body, mesh=mesh, in_specs=in_specs, out_specs=out_specs, check_vma=False)
```

profile of v0, /device:TPU:0, one launch (start us, length us, event | category | flops | bytes accessed | tf_op | source)
XLA Modules:
  0.0 284.5 jit_solution(2137502294490413980)
XLA Ops:
  6.5 0.0 all-gather.5.cloned.1.call-start
  6.5 0.7 all-gather.5.cloned.1.call-update
  7.3 0.0 all-gather.7.cloned.1.call-start
  7.3 23.4 %all-gather = f32[16,64,2]{1,2,0:T(2,128)S(1)} all-gather(f32[1,64,2]{1,2,0:T(2,128)} %bitcast.13), channel_id=1, replica_groups=mesh['grp'=2,'row'=4,'col'=4] {'row','col'}, dimensions={0}, use_global_device_ids=true | all-gather | bytes 8704 | tf_op jit(solution)/shard_map/all_gather | solution.py:11
  30.8 0.1 reshape.2
  30.8 56.4 %all-gather.5.cloned.1.call-done = f32[2,1024,1024]{2,1,0:T(8,128)} async-done(((f32[2,64,1024]{2,1,0:T(8,128)}), f32[2,1024,1024]{2,1,0:T(8,128)}) %all-gather.5.cloned.1.call-update) | async-done | bytes 8388624 | tf_op jit(solution)/shard_map/all_gather | solution.py:10
  87.2 12.5 %add_convert_fusion = bf16[2,1024,256]{2,1,0:T(8,128)(2,1)} fusion(f32[2,1024,256]{2,1,0:T(8,128)} %param.5, f32[2,1024,1024]{2,1,0:T(8,128)} %all-gather.5.cloned.1.call-done, f32[2,1024]{1,0:T(2,128)S(1)} %bitcast.12), kind=kOutput, calls=%fused_computation.5 | convolution fusion | flops 6448218112 | bytes 11542528 | tf_op jit(solution)/shard_map/brm,bms->brs/dot_general | solution.py:15
  99.7 0.0 all-gather.7.cloned.1.call-update
  99.7 0.0 all-gather.9.cloned.1.call-start
  99.8 0.7 all-gather.9.cloned.1.call-update
  100.5 0.0 reduce-scatter.2.cloned.1.call-start
  100.5 32.6 %all-gather.7.cloned.1.call-done = bf16[2,1024,1024]{2,1,0:T(8,128)(2,1)} async-done(((bf16[2,1024,256]{2,1,0:T(8,128)(2,1)}), bf16[2,1024,1024]{2,1,0:T(8,128)(2,1)}) %all-gather.7.cloned.1.call-update) | async-done | bytes 4194320 | tf_op jit(solution)/shard_map/all_gather | solution.py:27
  133.1 82.2 %all-gather.9.cloned.1.call-done = bf16[2,1024,1024]{2,1,0:T(8,128)(2,1)} async-done(((bf16[2,1024,256]{2,1,0:T(8,128)(2,1)}), bf16[2,1024,1024]{2,1,0:T(8,128)(2,1)}) %all-gather.9.cloned.1.call-update) | async-done | bytes 4194320 | tf_op jit(solution)/shard_map/all_gather | solution.py:25
  215.3 10.0 %convolution_bitcast_fusion = f32[1024,1024]{1,0:T(8,128)} fusion(bf16[2,1024,1024]{2,1,0:T(8,128)(2,1)} %all-gather.7.cloned.1.call-done, bf16[2,1024,1024]{2,1,0:T(8,128)(2,1)} %all-gather.9.cloned.1.call-done), kind=kOutput, calls=%fused_computation.4 | convolution fusion | flops 4294967296 | bytes 12582912 | tf_op jit(solution)/shard_map/dot_general | solution.py:26
  225.3 0.0 reduce-scatter.2.cloned.1.call-update
  225.3 52.7 %reduce-scatter.2.cloned.1.call-done = f32[512,1024]{1,0:T(8,128)} async-done(((f32[1024,1024]{1,0:T(8,128)}), f32[512,1024]{1,0:T(8,128)}) %reduce-scatter.2.cloned.1.call-update) | async-done | bytes 2097168 | tf_op jit(solution)/shard_map/reduce_scatter | solution.py:32
  (1 shorter events, 0.0 us)
Async XLA Ops:
  6.5 80.7 %all-gather.5.cloned.1.call-start = ((), (), s32[]{:S(2)}) async-start(), calls=%async_computation.1 | async-start | bytes 8912896 | tf_op jit(solution)/shard_map/all_gather | solution.py:10
  7.3 125.9 %all-gather.7.cloned.1.call-start = ((), (), s32[]{:S(2)}) async-start(), calls=%async_computation.2 | async-start | bytes 5242880 | tf_op jit(solution)/shard_map/all_gather | solution.py:27
  99.7 115.6 %all-gather.9.cloned.1.call-start = ((), (), s32[]{:S(2)}) async-start(), calls=%async_computation.3 | async-start | bytes 5242880 | tf_op jit(solution)/shard_map/all_gather | solution.py:25
  100.5 177.5 %reduce-scatter.2.cloned.1.call-start = ((), (), s32[]{:S(2)}) async-start(), calls=%async_computation.4 | async-start | bytes 6291456 | tf_op jit(solution)/shard_map/reduce_scatter | solution.py:32
Sparse Core Ops, SparseCore 0:
  9.5 77.6 all-gather.4
  99.8 33.2 all-gather.6
  134.7 80.5 all-gather.8
  225.5 52.4 reduce-scatter.1
where the time goes:
time: 285 us
  waiting for transfers between devices  225 us (79%)
  blocking collectives  23.4 us (8%)
  matrix products  22.5 us (8%)
  between operations  13.1 us (5%)
    all_gather x1, waiting for transfers between devices, body(): column_panel = lax.all_gather(projected, 'row', axis=2, tiled=True)  82.2 us
    all_gather x1, waiting for transfers between devices, body(): factor_piece = lax.all_gather(factor, ('row', 'col'), axis=1, tiled=True)  56.4 us
    reduce_scatter x1, waiting for transfers between devices, body(): summed = lax.psum_scatter(gram_tile, 'grp', scatter_dimension=0, tiled=True)  52.7 us
    all_gather x1, waiting for transfers between devices, body(): lax.all_gather(projected, 'col', axis=2, tiled=True)  32.6 us
    all_gather x1, blocking collectives, body(): pivot_piece = lax.all_gather(pivots, ('row', 'col'), axis=1, tiled=True)  23.4 us
    dot_general x1, matrix products, body(): jnp.einsum('brm,bms->brs', triangle, constraints, precision=exact_mode, p...  12.5 us
    dot_general x1, matrix products, body(): lax.dot_general(lax.all_gather(projected, 'col', axis=2, tiled=True), col...  10 us
  transfers between devices with their start and end apart: 4, of which 4 were waited for; matrix products, arithmetic and copies ran while one was open for 0% of the time, Pallas kernels for 0%

commit v1 on v0

--- a/solution.py
+++ b/solution.py
@@ -22,7 +22,26 @@
     scaled = pivot_piece[:, :, None] * constraints
     projected_full = product + scaled
     projected = projected_full.astype(jnp.bfloat16)
-    column_panel = lax.all_gather(projected, "row", axis=2, tiled=True)
+    size, mine, width = (lax.axis_size("row"), lax.axis_index("row"), projected.shape[2])
+    right = [(i, (i + 1) % size) for i in range(size)]
+    behind = [(i, (i - 1) % size) for i in range(size)]
+    whole = jnp.zeros(
+        (*projected.shape[:2], size * width, *projected.shape[2 + 1 :]), projected.dtype
+    )
+    whole = lax.dynamic_update_slice_in_dim(whole, projected, mine * width, axis=2)
+    from_left = from_right = projected
+    half = size // 2
+    for step in range(1, half + 1):
+        from_left = lax.ppermute(from_left, "row", right)
+        whole = lax.dynamic_update_slice_in_dim(
+            whole, from_left, (mine - step) % size * width, axis=2
+        )
+        if step < size - half:
+            from_right = lax.ppermute(from_right, "row", behind)
+            whole = lax.dynamic_update_slice_in_dim(
+                whole, from_right, (mine + step) % size * width, axis=2
+            )
+    column_panel = whole
     gram_tile = lax.dot_general(
         lax.all_gather(projected, "col", axis=2, tiled=True),
         column_panel,

time: 285 us -> 242 us (0.85)
  waiting for transfers between devices: 225 us -> 175 us
  local copies, waits for them, and re-layouts: 0.08 us -> 5.93 us
  starting transfers between devices: 0.12 us -> 3.96 us
    all_gather x1 -> x0, waiting for transfers between devices: 82.2 us -> none  [body(): column_panel = lax.all_gather(projected, 'row', axis=2, tiled=True)]
    ppermute x0 -> x3, waiting for transfers between devices: none -> 66.3 us  [the longest x2 46.8 us: body(): from_left = lax.ppermute(from_left, 'row', right)]
    all_gather x1, waiting for transfers between devices: 32.6 us -> 0.01 us  [body(): lax.all_gather(projected, 'col', axis=2, tiled=True)]
    ppermute x0 -> x3, starting transfers between devices: none -> 3.88 us  [the longest x1 2.94 us: body(): from_right = lax.ppermute(from_right, 'row', behind)]
    dynamic_update_slice x0 -> x3, local copies, waits for them, and re-layouts: none -> 3.35 us  [the longest x2 2.23 us: body(): lax.dynamic_update_slice_in_dim(whole, from_left, (mine - step) % size *...]
  transfers between devices with their start and end apart: 4 -> 6, of which waited for: 4 -> 5; matrix products, arithmetic and copies ran while one was open for 0% -> 1% of each run, Pallas kernels for 0% -> 0%
where the time goes in v1:
time: 242 us
  waiting for transfers between devices  175 us (72%)
  blocking collectives  23.4 us (10%)
  matrix products  20 us (8%)
  between operations  13.1 us (5%)
  local copies, waits for them, and re-layouts  5.93 us (2%)
  starting transfers between devices  3.96 us (2%)
    all_gather x1, waiting for transfers between devices, body(): factor_piece = lax.all_gather(factor, ('row', 'col'), axis=1, tiled=True)  56.4 us
    reduce_scatter x1, waiting for transfers between devices, body(): summed = lax.psum_scatter(gram_tile, 'grp', scatter_dimension=0, tiled=True)  52 us
    ppermute x2, waiting for transfers between devices, body(): from_left = lax.ppermute(from_left, 'row', right)  46.8 us
    all_gather x1, blocking collectives, body(): pivot_piece = lax.all_gather(pivots, ('row', 'col'), axis=1, tiled=True)  23.4 us
    ppermute x1, waiting for transfers between devices, body(): from_right = lax.ppermute(from_right, 'row', behind)  19.5 us
    dot_general x1, matrix products, body(): jnp.einsum('brm,bms->brs', triangle, constraints, precision=exact_mode, p...  10.1 us
    dot_general x1, matrix products, body(): lax.dot_general(lax.all_gather(projected, 'col', axis=2, tiled=True), col...  10 us
  transfers between devices with their start and end apart: 6, of which 5 were waited for; matrix products, arithmetic and copies ran while one was open for 1% of the time, Pallas kernels for 0%

profile of v1, /device:TPU:0, one launch (start us, length us, event | category | flops | bytes accessed | tf_op | source)
XLA Modules:
  0.0 241.9 jit_solution(11542675467153753420)
XLA Ops:
  6.5 0.0 copy-start
  6.5 0.0 all-gather.4.cloned.1.call-start
  6.5 0.7 all-gather.4.cloned.1.call-update
  7.3 0.0 all-gather.6.cloned.1.call-start
  7.3 23.4 %all-gather = f32[16,64,2]{1,2,0:T(2,128)S(1)} all-gather(f32[1,64,2]{1,2,0:T(2,128)} %bitcast.13), channel_id=1, replica_groups=mesh['grp'=2,'row'=4,'col'=4] {'row','col'}, dimensions={0}, use_global_device_ids=true | all-gather | bytes 8704 | tf_op jit(solution)/shard_map/all_gather | solution.py:11
  30.8 0.1 reshape.2
  30.8 56.4 %all-gather.4.cloned.1.call-done = f32[2,1024,1024]{2,1,0:T(8,128)} async-done(((f32[2,64,1024]{2,1,0:T(8,128)}), f32[2,1024,1024]{2,1,0:T(8,128)}) %all-gather.4.cloned.1.call-update) | async-done | bytes 8388624 | tf_op jit(solution)/shard_map/all_gather | solution.py:10
  87.2 2.5 %broadcast_in_dim.11 = bf16[2,1024,1024]{2,1,0:T(8,128)(2,1)} broadcast(bf16[]{:T(256)} %constant.31.clone.1), dimensions={} | broadcast | bytes 4194306 | tf_op jit(solution)/shard_map/broadcast_in_dim | solution.py:28
  89.7 0.0 copy-done
  89.7 10.1 %constant_dynamic-update-slice_fusion.3 = (bf16[2,1024,1024]{2,1,0:T(8,128)(2,1)}, bf16[2,1024,256]{2,1,0:T(8,128)(2,1)}) fusion(bf16[2,1024,1024]{2,1,0:T(8,128)(2,1)} %broadcast_in_dim.11, s32[]{:T(128)S(6)} %select_n.32, f32[2,1024,256]{2,1,0:T(8,128)S(1)} %copy-done, f32[2,1024]{1,0:T(2,128)S(1)} %bitcast.12, ...), kind=kOutput, calls=%fused_computation.9 | convolution fusion | flops 6448218112 | bytes 14688260 | tf_op jit(solution)/shard_map/brm,bms->brs/dot_general | solution.py:15
  99.8 0.0 all-gather.6.cloned.1.call-update
  99.8 0.0 reduce-scatter.2.cloned.1.call-start
  99.8 0.9 collective-permute-start
  100.8 2.9 %collective-permute-start.1 = (bf16[2,1024,256]{2,1,0:T(8,128)(2,1)}, bf16[2,1024,256]{2,1,0:T(8,128)(2,1)S(1)}, u32[]{:S(2)}, u32[]{:S(2)}) collective-permute-start(bf16[2,1024,256]{2,1,0:T(8,128)(2,1)} %get-tuple-element.6), channel_id=1, source_target_pairs={{0,12},{4,0},{8,4},{12,8},{1,13},{5,1},{9,5},{13,9},{2,14},{6,2},{... | collective-permute-start | bytes 3145736 | tf_op jit(solution)/shard_map/ppermute | solution.py:40
  103.7 24.2 %collective-permute-done = bf16[2,1024,256]{2,1,0:T(8,128)(2,1)S(1)} collective-permute-done((bf16[2,1024,256]{2,1,0:T(8,128)(2,1)}, bf16[2,1024,256]{2,1,0:T(8,128)(2,1)S(1)}, u32[]{:S(2)}, u32[]{:S(2)}) %collective-permute-start) | collective-permute-done | bytes 1048608 | tf_op jit(solution)/shard_map/ppermute | solution.py:35
  127.9 0.0 collective-permute-start.2
  127.9 1.1 constant_dynamic-update-slice_fusion.2
  129.0 19.5 %collective-permute-done.1 = bf16[2,1024,256]{2,1,0:T(8,128)(2,1)S(1)} collective-permute-done((bf16[2,1024,256]{2,1,0:T(8,128)(2,1)}, bf16[2,1024,256]{2,1,0:T(8,128)(2,1)S(1)}, u32[]{:S(2)}, u32[]{:S(2)}) %collective-permute-start.1) | collective-permute-done | bytes 1048608 | tf_op jit(solution)/shard_map/ppermute | solution.py:40
  148.5 1.1 constant_dynamic-update-slice_fusion.1
  149.6 22.6 %collective-permute-done.2 = bf16[2,1024,256]{2,1,0:T(8,128)(2,1)S(1)} collective-permute-done((bf16[2,1024,256]{2,1,0:T(8,128)(2,1)S(1)}, bf16[2,1024,256]{2,1,0:T(8,128)(2,1)S(1)}, u32[]{:S(2)}, u32[]{:S(2)}) %collective-permute-start.2) | collective-permute-done | bytes 1048608 | tf_op jit(solution)/shard_map/ppermute | solution.py:35
  172.2 1.1 constant_dynamic-update-slice_fusion
  173.3 0.0 all-gather.6.cloned.1.call-done
  173.3 10.0 %convolution_bitcast_fusion = f32[1024,1024]{1,0:T(8,128)} fusion(bf16[2,1024,1024]{2,1,0:T(8,128)(2,1)} %all-gather.6.cloned.1.call-done, bf16[2,1024,1024]{2,1,0:T(8,128)(2,1)} %constant_dynamic-update-slice_fusion), kind=kOutput, calls=%fused_computation.4 | convolution fusion | flops 4294967296 | bytes 12582912 | tf_op jit(solution)/shard_map/dot_general | solution.py:45
  183.3 0.0 reduce-scatter.2.cloned.1.call-update
  183.3 52.0 %reduce-scatter.2.cloned.1.call-done = f32[512,1024]{1,0:T(8,128)} async-done(((f32[1024,1024]{1,0:T(8,128)}), f32[512,1024]{1,0:T(8,128)}) %reduce-scatter.2.cloned.1.call-update) | async-done | bytes 2097168 | tf_op jit(solution)/shard_map/reduce_scatter | solution.py:51
  (1 shorter events, 0.0 us)
Async XLA Ops:
  6.5 83.2 %copy-start = (f32[2,1024,256]{2,1,0:T(8,128)S(1)}, f32[2,1024,256]{2,1,0:T(8,128)}, u32[]{:S(2)}) copy-start(f32[2,1024,256]{2,1,0:T(8,128)} %param.5) | copy-start | bytes 6291460
  6.5 80.7 %all-gather.4.cloned.1.call-start = ((), (), s32[]{:S(2)}) async-start(), calls=%async_computation.1 | async-start | bytes 8912896 | tf_op jit(solution)/shard_map/all_gather | solution.py:10
  7.3 166.1 %all-gather.6.cloned.1.call-start = ((), (), s32[]{:S(2)}) async-start(), calls=%async_computation.2 | async-start | bytes 5242880 | tf_op jit(solution)/shard_map/all_gather | solution.py:46
  99.8 135.5 %reduce-scatter.2.cloned.1.call-start = ((), (), s32[]{:S(2)}) async-start(), calls=%async_computation.3 | async-start | bytes 6291456 | tf_op jit(solution)/shard_map/reduce_scatter | solution.py:51
  99.8 28.1 %collective-permute-start = (bf16[2,1024,256]{2,1,0:T(8,128)(2,1)}, bf16[2,1024,256]{2,1,0:T(8,128)(2,1)S(1)}, u32[]{:S(2)}, u32[]{:S(2)}) collective-permute-start(bf16[2,1024,256]{2,1,0:T(8,128)(2,1)} %get-tuple-element.6), channel_id=1, source_target_pairs={{0,4},{4,8},{8,12},{12,0},{1,5},{5,9},{9,13},{13,1},{2,6},{6,10},{... | collective-permute-start | bytes 3145736 | tf_op jit(solution)/shard_map/ppermute | solution.py:35
  100.8 47.7 %collective-permute-start.1 = (bf16[2,1024,256]{2,1,0:T(8,128)(2,1)}, bf16[2,1024,256]{2,1,0:T(8,128)(2,1)S(1)}, u32[]{:S(2)}, u32[]{:S(2)}) collective-permute-start(bf16[2,1024,256]{2,1,0:T(8,128)(2,1)} %get-tuple-element.6), channel_id=1, source_target_pairs={{0,12},{4,0},{8,4},{12,8},{1,13},{5,1},{9,5},{13,9},{2,14},{6,2},{... | collective-permute-start | bytes 3145736 | tf_op jit(solution)/shard_map/ppermute | solution.py:40
  127.9 44.3 %collective-permute-start.2 = (bf16[2,1024,256]{2,1,0:T(8,128)(2,1)S(1)}, bf16[2,1024,256]{2,1,0:T(8,128)(2,1)S(1)}, u32[]{:S(2)}, u32[]{:S(2)}) collective-permute-start(bf16[2,1024,256]{2,1,0:T(8,128)(2,1)S(1)} %collective-permute-done), channel_id=1, source_target_pairs={{0,4},{4,8},{8,12},{12,0},{1,5},{5,9},{9,13},{13,1},{2,6},{6,10},{... | collective-permute-start | bytes 3145736 | tf_op jit(solution)/shard_map/ppermute | solution.py:35
Sparse Core Ops, SparseCore 0:
  9.5 77.6 all-gather.3
  99.9 33.2 all-gather.5
  183.5 51.8 reduce-scatter.1
